TPU v7x, 1024 devices: a whole 4x8x16 slice. The times are simulated.
1024 devices in a mesh: rhs: 64 (over z, x), clus: 16 (over y, core).
Axes of the slice: x: 4, y: 8, z: 16, core: 2. Of those that a mesh axis runs over, the one named last changes fastest.
Arguments:
- incident: bfloat16 [6656, 131072], P('rhs', 'clus'), may hold values from -6 to 6
- v_factors: bfloat16 [80, 2048, 128], P('clus', 'rhs'), may hold values from -0.125 to 0.125
- u_factors: bfloat16 [160, 2048, 128], P('clus', 'rhs'), may hold values from -0.5 to 0.5
- block_source: int32 [80], P('clus'), may hold values from 0 to 3
- block_rank: int32 [80], P('clus'), may hold values from 16 to 128
- block_slot: int32 [80], P('clus'), may hold values from 0 to 159, as said below
- slot_target: int32 [160], P('clus'), may hold values from 0 to 3
Outputs:
- scattered: bfloat16 [6656, 131072], P('rhs', 'clus')
Inputs may be any that keep to these rules, and one draw needn't show every extreme that they name: `block_slot`: every value is a slot number, all 80 values are distinct, and slot v belongs to index v // 10 of clus. The 5 blocks of one index of clus name at most 1 slots of any one index, and in every draw some index sends exactly 1 to one index and some index of clus receives exactly 10 blocks. Which slots stay empty varies.
All inputs are finite; a program needn't handle non-finite values.
Results may differ from a plain program's by a relative error of at most 0.0049.
Values may be sent and summed in bfloat16 or wider, within the bound.
A program may use at most 64 MiB of HBM per device.

v0:
```python
import jax
import jax.numpy as jnp
from jax import lax
from jax.sharding import Mesh
from jax.sharding import PartitionSpec as P

RHS = ("rhs_0", "rhs_1")


def whole_of(shard, axes, dim):
    whole = shard
    for number in range(len(axes) - 1, -1, -1):
        whole = lax.all_gather(whole, axes[number], axis=dim, tiled=True)
    return whole


def local(incident, v_factors, u_factors, block_source, block_rank, block_slot, slot_target):
    columns = incident.shape[0]
    blocks = v_factors.shape[0]
    rank_max = v_factors.shape[2]
    capacity = u_factors.shape[0]
    devices = lax.axis_size("clus")
    cluster_len = v_factors.shape[1] * lax.axis_size(RHS)
    local_clusters = incident.shape[1] // cluster_len
    per_peer = max(1, (2 * blocks + devices - 1) // devices)
    sources = jnp.take(incident.reshape(columns, local_clusters, cluster_len), block_source, axis=1)
    compressed = jnp.einsum(
        "cbr,brk->bck", sources, whole_of(v_factors, RHS, 1), preferred_element_type=jnp.float32
    )
    rank_index = lax.broadcasted_iota(jnp.int32, (blocks, 1, rank_max), 2)
    compressed = jnp.where(rank_index < block_rank[:, None, None], compressed, 0.0).astype(
        jnp.bfloat16
    )
    target_dev = block_slot // capacity
    target_pos = block_slot % capacity
    later_index = lax.broadcasted_iota(jnp.int32, (blocks, blocks), 0)
    earlier_index = lax.broadcasted_iota(jnp.int32, (blocks, blocks), 1)
    same_target = target_dev[None, :] == target_dev[:, None]
    before = jnp.sum((same_target & (earlier_index < later_index)).astype(jnp.int32), axis=1)
    position = target_dev * per_peer + before
    places = lax.broadcasted_iota(jnp.int32, (blocks, devices * per_peer), 1)
    placed = position[:, None] == places
    outgoing = jnp.einsum(
        "bp,bck->pck", placed.astype(jnp.bfloat16), compressed, preferred_element_type=jnp.float32
    ).astype(jnp.bfloat16)
    labels = jnp.sum(jnp.where(placed, target_pos[:, None] + 1, 0), axis=0) - 1
    arrived, arrived_labels = (
        lax.all_to_all(outgoing, "clus", split_axis=0, concat_axis=0, tiled=True),
        lax.all_to_all(labels, "clus", split_axis=0, concat_axis=0, tiled=True),
    )
    slot_ids = lax.broadcasted_iota(jnp.int32, (devices * per_peer, capacity), 1)
    landing = (arrived_labels[:, None] == slot_ids).astype(jnp.bfloat16)
    slot_rows = jnp.einsum(
        "pj,pck->jck", landing, arrived, preferred_element_type=jnp.float32
    ).astype(jnp.bfloat16)
    cluster_ids = lax.broadcasted_iota(jnp.int32, (capacity, local_clusters), 1)
    owners = (slot_target[:, None] == cluster_ids).astype(jnp.float32)
    products = jnp.einsum(
        "jck,jrk->jcr",
        slot_rows,
        lax.all_gather(u_factors, RHS, axis=1, tiled=True),
        preferred_element_type=jnp.float32,
    )
    summed = jnp.einsum("jt,jcr->ctr", owners, products, precision=lax.Precision.HIGHEST)
    return summed.reshape(columns, local_clusters * cluster_len).astype(jnp.bfloat16)


def solution(mesh):
    torus = Mesh(mesh.devices.reshape(16, 4, mesh.shape["clus"]), ("rhs_0", "rhs_1", "clus"))
    return jax.shard_map(
        local,
        mesh=torus,
        in_specs=(
            P(RHS, "clus"),
            P("clus", RHS, None),
            P("clus", RHS, None),
            P("clus"),
            P("clus"),
            P("clus"),
            P("clus"),
        ),
        out_specs=P(RHS, "clus"),
        check_vma=False,
    )
```

profile of v0, /device:TPU:8, one launch (start us, length us, event | category | flops | bytes accessed | tf_op | source)
XLA Modules:
  0.0 291.4 jit_solution(11434818019935854118)
XLA Ops:
  6.5 0.0 copy-start.1
  6.5 0.0 all-gather.3.cloned.1.call-start
  6.5 14.1 %all_gather.9 = bf16[5,128,128]{2,1,0:T(8,128)(2,1)} all-gather(bf16[5,32,128]{2,1,0:T(8,128)(2,1)} %param.8), channel_id=1, replica_groups=mesh['rhs_0'=16,'rhs_1'=4,'clus'=16] {'rhs_1'}, dimensions={1}, use_global_device_ids=true | all-gather | bytes 204800 | tf_op jit(solution)/shard_map/all_gather | solution.py:13
  20.6 0.0 all-gather.3.cloned.1.call-update
  20.6 0.0 all-gather.5.cloned.1.call-start
  20.7 0.7 all-gather.5.cloned.1.call-update
  21.4 0.7 fusion.30
  22.0 0.2 convert_reduce_fusion
  22.2 0.1 select_reduce_fusion
  22.3 0.7 copy.26
  23.0 15.4 %all-to-all-start = ((s32[16,1,1]{2,1,0:T(1,128)}), s32[16,1,1]{2,1,0:T(1,128)S(1)}, u32[]{:S(2)}, u32[]{:S(2)}) async-start(s32[16,1,1]{2,1,0:T(1,128)} %copy.26), calls=%async_computation | async-start | bytes 16384 | tf_op jit(solution)/shard_map/all_to_all | solution.py:49
  38.4 1.6 copy.46
  40.0 0.0 copy-done.1
  40.1 0.0 copy-start.2
  40.1 2.2 gather_fusion
  42.3 0.0 copy-done.2
  42.3 0.1 iota_compare_fusion.1
  42.4 62.8 %all-gather.3.cloned.1.call-done = bf16[5,2048,128]{2,1,0:T(8,128)(2,1)} async-done(((bf16[5,128,128]{2,1,0:T(8,128)(2,1)}), bf16[5,2048,128]{2,1,0:T(8,128)(2,1)}) %all-gather.3.cloned.1.call-update) | async-done | bytes 2621456 | tf_op jit(solution)/shard_map/all_gather | solution.py:13
  105.1 3.3 %fusion.12 = bf16[5,104,128]{2,1,0:T(8,128)(2,1)S(1)} fusion(bf16[5,2048,128]{2,1,0:T(8,128)(2,1)} %all-gather.3.cloned.1.call-done, bf16[5,104,2048]{2,1,0:T(8,128)(2,1)} %gather_fusion, pred[5]{0:T(512)(128)(4,1)S(1)} %compare_and_fusion, pred[5,128]{1,0:T(8,128)(4,1)S(1)} %iota_compare_fusion.1), kind=kOutput, calls=%fused_computation.12 | convolution fusion | flops 273827840 | bytes 4885125 | tf_op jit(solution)/shard_map/cbr,brk->bck/dot_general | solution.py:27
  108.5 0.4 convolution_convert_fusion
  108.9 0.9 copy.29
  109.8 0.0 all-to-all-done
  109.8 7.3 %all-to-all-start.1 = ((bf16[16,104,128]{2,1,0:T(8,128)(2,1)}), bf16[16,104,128]{2,1,0:T(8,128)(2,1)S(1)}, u32[]{:S(2)}, u32[]{:S(2)}) async-start(bf16[16,104,128]{2,1,0:T(8,128)(2,1)} %copy.29), calls=%async_computation.1 | async-start | bytes 851968 | tf_op jit(solution)/shard_map/all_to_all | solution.py:48
  117.1 0.4 reduce
  117.5 12.1 %all-to-all-done.1 = bf16[16,104,128]{2,1,0:T(8,128)(2,1)S(1)} async-done(((bf16[16,104,128]{2,1,0:T(8,128)(2,1)}), bf16[16,104,128]{2,1,0:T(8,128)(2,1)S(1)}, u32[]{:S(2)}, u32[]{:S(2)}) %all-to-all-start.1) | async-done | bytes 426016 | tf_op jit(solution)/shard_map/all_to_all | solution.py:48
  129.6 0.3 convolution_convert_fusion.1
  129.8 0.0 copy-start
  129.9 133.5 %all-gather.5.cloned.1.call-done = bf16[10,2048,128]{2,1,0:T(8,128)(2,1)} async-done(((bf16[10,32,128]{2,1,0:T(8,128)(2,1)}), bf16[10,2048,128]{2,1,0:T(8,128)(2,1)}) %all-gather.5.cloned.1.call-update) | async-done | bytes 5242896 | tf_op jit(solution)/shard_map/all_gather | solution.py:61
  263.4 5.8 %fusion.17 = f32[10,104,2048]{2,1,0:T(8,128)S(1)} fusion(bf16[10,2048,128]{2,1,0:T(8,128)(2,1)} %all-gather.5.cloned.1.call-done, bf16[10,104,128]{2,0,1:T(8,128)(2,1)S(1)} %convolution_convert_fusion.1), kind=kOutput, calls=%fused_computation.15 | convolution fusion | flops 545259520 | bytes 14028800 | tf_op jit(solution)/shard_map/jck,jrk->jcr/dot_general | solution.py:58
  269.1 0.0 copy-done
  269.2 13.1 %fusion.2 = bf16[104,2048,4]{1,2,0:T(4,128)(2,1)S(1)} fusion(f32[10,104,2048]{2,1,0:T(8,128)S(1)} %fusion.17, s32[10]{0:T(128)S(1)} %copy-done), kind=kOutput, calls=%fused_computation.3 | convolution fusion | flops 103088168 | bytes 10223656 | tf_op jit(solution)/shard_map/jt,jcr->ctr/dot_general | solution.py:64
  282.3 2.3 copy.34
  (5 shorter events, 0.0 us)
Async XLA Ops:
  6.5 33.5 %copy-start.1 = (s32[5]{0:T(128)S(1)}, s32[5]{0:T(128)}, u32[]{:S(2)}) copy-start(s32[5]{0:T(128)} %param.10) | copy-start | bytes 64
  6.5 98.6 %all-gather.3.cloned.1.call-start = ((), (), s32[]{:S(2)}) async-start(), calls=%async_computation.2 | async-start | bytes 2785280 | tf_op jit(solution)/shard_map/all_gather | solution.py:13
  20.6 242.8 %all-gather.5.cloned.1.call-start = ((), (), s32[]{:S(2)}) async-start(), calls=%async_computation.3 | async-start | bytes 5324800 | tf_op jit(solution)/shard_map/all_gather | solution.py:61
  23.0 86.8 %all-to-all-start = ((s32[16,1,1]{2,1,0:T(1,128)}), s32[16,1,1]{2,1,0:T(1,128)S(1)}, u32[]{:S(2)}, u32[]{:S(2)}) async-start(s32[16,1,1]{2,1,0:T(1,128)} %copy.26), calls=%async_computation | async-start | bytes 16384 | tf_op jit(solution)/shard_map/all_to_all | solution.py:49
  40.1 2.2 copy-start.2
  109.8 19.8 %all-to-all-start.1 = ((bf16[16,104,128]{2,1,0:T(8,128)(2,1)}), bf16[16,104,128]{2,1,0:T(8,128)(2,1)S(1)}, u32[]{:S(2)}, u32[]{:S(2)}) async-start(bf16[16,104,128]{2,1,0:T(8,128)(2,1)} %copy.29), calls=%async_computation.1 | async-start | bytes 851968 | tf_op jit(solution)/shard_map/all_to_all | solution.py:48
  129.8 139.3 %copy-start = (s32[10]{0:T(128)S(1)}, s32[10]{0:T(128)}, u32[]{:S(2)}) copy-start(s32[10]{0:T(128)} %param.13) | copy-start | bytes 124
Sparse Core Ops, SparseCore 0:
  20.7 84.3 all-gather.2
  109.2 154.1 all-gather.4
where the time goes:
time: 292 us; the launch traced here: 291 us
  waiting for transfers between devices  209 us (72%)
  matrix products  22.9 us (8%)
  starting transfers between devices  22.7 us (8%)
  blocking collectives  14.1 us (5%)
  between operations  13.5 us (5%)
  local copies, waits for them, and re-layouts  7.7 us (3%)
    all_gather x1, waiting for transfers between devices, local(): lax.all_gather(u_factors, RHS, axis=1, tiled=True)  134 us
    all_gather x1, waiting for transfers between devices, whole_of(): whole = lax.all_gather(whole, axes[number], axis=dim, tiled=True)  62.8 us
    all_to_all x1, starting transfers between devices, local(): lax.all_to_all(labels, 'clus', split_axis=0, concat_axis=0, tiled=True)  15.4 us
    all_gather x1, blocking collectives, whole_of(): whole = lax.all_gather(whole, axes[number], axis=dim, tiled=True)  14.1 us
    dot_general x1, matrix products, local(): jnp.einsum('jt,jcr->ctr', owners, products, precision=lax.Precision.HIGHEST)  13.1 us
    all_to_all x1, waiting for transfers between devices, local(): lax.all_to_all(outgoing, 'clus', split_axis=0, concat_axis=0, tiled=True)  12.1 us
    all_to_all x1, starting transfers between devices, local(): lax.all_to_all(outgoing, 'clus', split_axis=0, concat_axis=0, tiled=True)  7.29 us
  transfers between devices with their start and end apart: 4, of which 3 were waited for; matrix products, arithmetic and copies ran while one was open for 4% of the time, Pallas kernels for 0%

commit v1 on v0

v1 whole, which is shorter than its diff:
```python
import functools

import jax
import jax.numpy as jnp
from jax import lax
from jax.experimental import pallas as pl
from jax.experimental.pallas import tpu as pltpu
from jax.sharding import Mesh
from jax.sharding import PartitionSpec as P

MESH = pl.DeviceIdType.MESH
NZ, NX, NC = 16, 4, 16
HALF = NZ // 2
BLOCKS, SLOTS, CLUSTERS = 5, 10, 4
COLS, ROWS, R, CL = 104, 32, 128, 2048
GROUP = NX * ROWS
PAD = 112
V_PARTS, V_A = ((0, 1),), 1
U_PARTS, U_A = ((0, 1), (1, 2), (2, 3), (3, 4), (4, 5)), 5
PER_HOP, SELECT_AT = 3, 5
V_LAG, U_LAG = 3, 2


def schedule():
    flow = [("UX", 0, 0)]
    for s in range(HALF + 1):
        flow += [("U", s, i) for i in range(len(U_PARTS))]
        if s > 0:
            flow.append(("U", s, -1))
        if s > U_LAG:
            flow.append(("X", s - U_LAG, 0))
    flow += [("X", s, 0) for s in range(HALF - U_LAG + 1, HALF + 1)]
    ops = [("V0", 0, 0), ("U0", 0, 0), ("VX", 0, 0)]
    for h in range(1, HALF + 1):
        ops += [("V", h, i) for i in (*range(len(V_PARTS)), -1)]
        ops, flow = ops + flow[:PER_HOP], flow[PER_HOP:]
        ops += [("W", h - V_LAG, 0)] if h > V_LAG else []
        ops += [("G", 0, 0)] if h == 2 else []
        ops += [("P", h - V_LAG - 2, 0)] if h > V_LAG + 2 else []
    for h in range(HALF - V_LAG + 1, HALF + 1):
        ops += [("W", h, 0), *flow[:2], ("P", h - 2, 0)]
        flow = flow[2:]
    ops += [("P", HALF - 1, 0), *flow[:1], ("P", HALF, 0), ("C", 0, 0)]
    flow = flow[1:]
    ready = 0
    chosen = False
    for op in (*flow, ("END", 0, 0)):
        kind, s, i = op
        if not chosen and (kind == "END" or (kind == "X" and s == SELECT_AT)):
            ops += [("L", 0, 0), ("S", 0, 0)]
            chosen = True
        if kind == "END":
            ops += [("E", e, 0) for e in range(ready + 1, HALF + 1)]
            break
        ops.append(op)
        if chosen and kind == "X":
            upto = s - 1
            ops += [("E", e, 0) for e in range(ready + 1, upto + 1)]
            ready = max(ready, upto)
    return ops


PEERS = (8, 7, 9, 6, 10, 5, 11, 4, 12, 3, 13, 2, 14, 1, 15)


class Names:
    def __init__(self):
        self.number = {}

    def __call__(self, *name):
        return self.number.setdefault(name, len(self.number))


def kernel(
    x_hbm, v_hbm, u_hbm, source_hbm, rank_hbm, slot_hbm, target_hbm, out_hbm,
    x_ref, windows, gv, gu, acc, packed, outgoing, arrived, left, out_ref, mine, theirs,
    to_window, to_peer, to_slot, to_owner, source, rank, slot, target, recv, send, local, store,
):
    z, x, c = lax.axis_index("rhs_0"), lax.axis_index("rhs_1"), lax.axis_index("clus")
    up, down = {"rhs_0": lax.rem(z + 1, NZ)}, {"rhs_0": lax.rem(z + NZ - 1, NZ)}
    side = {k: {"rhs_1": lax.rem(x + k, NX)} for k in (1, 2, 3)}
    peer = {k: {"clus": lax.rem(c + k, NC)} for k in range(1, NC)}
    number = Names()
    sent, stores, early = [], [], []

    def remote(name, src, dst, device):
        i = number(*name)
        return pltpu.make_async_remote_copy(
            src_ref=src,
            dst_ref=dst,
            send_sem=send.at[i],
            recv_sem=recv.at[i],
            device_id=device,
            device_id_type=MESH,
        )

    def push(name, src, dst, device):
        copy = remote(name, src, dst, device)
        copy.start()
        sent.append(copy)

    def drain(last):
        while len(early) < last:
            sent[len(early)].wait_send()
            early.append(True)

    def landed(name, dst):
        remote(name, dst, dst, up).wait_recv()

    def rows(k, start=0, size=ROWS):
        first = lax.rem(x + k, NX) * ROWS + start
        return pl.ds(pl.multiple_of(first, 16), size)

    x_copies = [
        pltpu.make_async_copy(
            x_hbm.at[:, t * CL : (t + 1) * CL], x_ref.at[t, :COLS, :], local.at[9 + t]
        )
        for t in range(CLUSTERS)
    ]
    v_copy = pltpu.make_async_copy(v_hbm, gv.at[0, :, rows(0), :], local.at[1])
    u_copy = pltpu.make_async_copy(u_hbm, gu.at[0, :, rows(0), :], local.at[2])
    small = [
        pltpu.make_async_copy(a, b, local.at[3 + i])
        for i, (a, b) in enumerate(
            ((slot_hbm, slot), (source_hbm, source), (rank_hbm, rank), (target_hbm, target))
        )
    ]
    for copy in (*small, v_copy, u_copy, *x_copies):
        copy.start()

    barrier = pltpu.get_barrier_semaphore()
    partners = [up, down, *side.values(), *peer.values()]
    for device in partners:
        pl.semaphore_signal(barrier, inc=1, device_id=device, device_id_type=MESH)
    for t in range(CLUSTERS):
        x_ref[t, COLS:, :] = jnp.zeros((PAD - COLS, CL), jnp.bfloat16)
    for k in range(NC):
        arrived[k, COLS:, :] = jnp.zeros((PAD - COLS, R), jnp.bfloat16)
    pl.semaphore_wait(barrier, len(partners))

    streams = {
        "V": (gv, v_hbm, BLOCKS, V_PARTS, V_A),
        "U": (gu, u_hbm, SLOTS, U_PARTS, U_A),
    }

    def begin(f):
        full, own, count, _, cut = streams[f]
        for k in (1, 3, 2):
            push((f, "x0", k), own, full.at[0, :, rows(0), :], side[k])
        push((f, "z+", 1, -1), own.at[cut:], full.at[NZ - 1, cut:, rows(0), :], up)
        push((f, "z-", 1, -1), own.at[cut:], full.at[1, cut:, rows(0), :], down)

    def begin_x(f):
        full, _, _, _, _ = streams[f]
        for k in (1, 3, 2):
            landed((f, "x0", k), full.at[0, :, rows(NX - k), :])

    def spread(f, d):
        full, _, _, _, cut = streams[f]
        for k in (1, 3):
            ref = full.at[d, cut:, rows(0), :]
            push((f, "x", d, k), ref, ref, side[k])

    def step(f, s, i):
        full, _, _, parts, cut = streams[f]
        last, following = s == HALF, s + 1 == HALF
        for sign in "+-":
            d = (NZ - s if sign == "+" else s) % NZ
            onward = (NZ - s - 1 if sign == "+" else s + 1) % NZ
            device = up if sign == "+" else down
            half = 0 if sign == "+" else 1

            def place(part):
                if i >= 0:
                    size = GROUP // 2 if part else GROUP
                    return slice(*parts[i]), pl.ds(half * size if part else 0, size)
                return slice(cut, None), (rows(0, half * (ROWS // 2), ROWS // 2) if part else rows(0))

            if s > 0:
                landed((f, "z" + sign, s, i), full.at[(d, *place(last))])
            if not last:
                push(
                    (f, "z" + sign, s + 1, i),
                    full.at[(d, *place(following))],
                    full.at[(onward, *place(following))],
                    device,
                )
                if i < 0:
                    spread(f, d)
        if last and i < 0:
            spread(f, HALF)

    def pair(s):
        return (HALF,) if s == HALF else (NZ - s, s)

    def sideways(f, s):
        full, _, _, _, cut = streams[f]
        for d in pair(s):
            for k, half in ((1, 0), (3, 1)):
                landed((f, "x", d, k), full.at[d, cut:, rows(NX - k), :])
                ref = full.at[d, cut:, rows(NX - k, half * (ROWS // 2), ROWS // 2), :]
                push((f, "far", d, k), ref, ref, side[k])

    def complete(f, s):
        full, _, _, _, cut = streams[f]
        for d in pair(s):
            for k, half in ((1, 0), (3, 1)):
                ref = full.at[d, cut:, rows(2, half * (ROWS // 2), ROWS // 2), :]
                landed((f, "far", d, k), ref)

    def column(d):
        return lax.rem(z + d, NZ) * GROUP

    def one_hot(value, wanted):
        hit = jnp.full((16, 128), value, jnp.int32) == wanted
        return jnp.where(hit, 1.0, 0.0).astype(jnp.bfloat16)

    def make_labels():
        for copy in small:
            copy.wait()
        for k in range(NC):
            label = jnp.full((16, 128), -1, jnp.int32)
            for b in range(BLOCKS):
                device = jnp.full((16, 128), lax.div(slot[b], SLOTS), jnp.int32)
                place = jnp.full((16, 128), lax.rem(slot[b], SLOTS), jnp.int32)
                label = jnp.where(device == lax.rem(c + k, NC), place, label)
            if k == 0:
                theirs[0] = label
            else:
                mine[k] = label

    def tables():
        for b in range(BLOCKS):
            for t in range(CLUSTERS):
                to_window[b * CLUSTERS + t] = one_hot(source[b], t)
        for b in range(BLOCKS):
            device = lax.div(slot[b], SLOTS)
            for k in range(NC):
                to_peer[k * BLOCKS + b] = one_hot(device, lax.rem(c + k, NC))
        for j in range(SLOTS):
            for t in range(CLUSTERS):
                to_owner[j * CLUSTERS + t] = one_hot(target[j], t)

    def mix(weights, first, tiles):
        total = None
        for i, tile in enumerate(tiles):
            term = weights[first + i] * tile
            total = term if total is None else total + term
        return total

    def compress(s):
        complete("V", s)
        one, two = (0, HALF) if s == HALF else (NZ - s, s)
        places = [pl.ds(pl.multiple_of(column(d), GROUP), GROUP) for d in (one, two)]

        @pl.loop(0, PAD // 16)
        def _(i):
            row = pl.ds(pl.multiple_of(i * 16, 16), 16)
            for n, place in enumerate(places):
                tiles = [x_ref[t, row, place] for t in range(CLUSTERS)]
                for b in range(BLOCKS):
                    windows[b, row, n * GROUP : (n + 1) * GROUP] = mix(to_window, b * CLUSTERS, tiles)

        for b in range(BLOCKS):
            factor = jnp.concatenate([gv[one, b], gv[two, b]], axis=0)
            product = jnp.dot(windows[b], factor, preferred_element_type=jnp.float32)
            acc[b] = product if s == 1 else acc[b] + product

    def dispatch():
        k_index = lax.broadcasted_iota(jnp.int32, (PAD, R), 1)
        for b in range(BLOCKS):
            packed[b] = jnp.where(k_index < rank[b], acc[b], 0.0).astype(jnp.bfloat16)

        @pl.loop(0, PAD // 16)
        def _(i):
            row = pl.ds(pl.multiple_of(i * 16, 16), 16)
            tiles = [packed[b, row, :] for b in range(BLOCKS)]
            for k in range(1, NC):
                outgoing[k, row, :] = mix(to_peer, k * BLOCKS, tiles)
            arrived[0, row, :] = mix(to_peer, 0, tiles)

        for k in PEERS:
            push(("rows", k), outgoing.at[k, :COLS, :], arrived.at[k, :COLS, :], peer[k])

    def read_labels():
        for k in PEERS:
            landed(("label", k), theirs.at[k])
        for k in range(NC):
            label = theirs[k]
            for j in range(SLOTS):
                to_slot[j * NC + k] = jnp.where(label == j, 1.0, 0.0).astype(jnp.bfloat16)

    def select():
        for k in PEERS:
            landed(("rows", k), arrived.at[k, :COLS, :])

        @pl.loop(0, PAD // 16)
        def _(i):
            row = pl.ds(pl.multiple_of(i * 16, 16), 16)
            tiles = [arrived[k, row, :] for k in range(NC)]
            for j in range(SLOTS):
                values = mix(to_slot, j * NC, tiles)
                for t in range(CLUSTERS):
                    place = pl.ds(pl.multiple_of(t * PAD + i * 16, 16), 16)
                    left[place, j * R : (j + 1) * R] = to_owner[j * CLUSTERS + t] * values

    def expand(s):
        complete("U", s)
        one, two = (0, HALF) if s == HALF else (NZ - s, s)
        total = None
        for j in range(0, SLOTS, 2):
            right = jnp.concatenate(
                [jnp.concatenate([gu[d, j], gu[d, j + 1]], axis=1) for d in (one, two)], axis=0
            )
            product = lax.dot_general(
                left[:, j * R : (j + 2) * R],
                right,
                (((1,), (1,)), ((), ())),
                preferred_element_type=jnp.float32,
            )
            total = product if total is None else total + product
        rounded = total.astype(jnp.bfloat16)
        for t in range(CLUSTERS):
            for i, d in enumerate((one, two)):
                place = pl.ds(pl.multiple_of(t * CL + column(d), GROUP), GROUP)
                out_ref[:, place] = rounded[t * PAD : t * PAD + COLS, i * GROUP : (i + 1) * GROUP]
                copy = pltpu.make_async_copy(
                    out_ref.at[:, place], out_hbm.at[:, place], store.at[(s - 1) * 8 + t * 2 + i]
                )
                copy.start()
                stores.append(copy)

    marks = []
    for kind, s, i in schedule():
        if kind == "V0":
            begin("V")
            make_labels()
        elif kind == "U0":
            begin("U")
        elif kind == "VX":
            v_copy.wait()
            begin_x("V")
            for p in range(len(V_PARTS)):
                step("V", 0, p)
            for k in PEERS:
                push(("label", k), mine.at[k], theirs.at[k], peer[k])
            tables()
        elif kind == "UX":
            u_copy.wait()
            begin_x("U")
        elif kind == "G":
            for copy in x_copies:
                copy.wait()
        elif kind in "VU":
            step(kind, s, i)
        elif kind == "W":
            sideways("V", s)
        elif kind == "X":
            sideways("U", s)
        elif kind == "P":
            compress(s)
        elif kind == "C":
            dispatch()
            marks.insert(0, len(sent))
        elif kind == "L":
            read_labels()
            drain(marks[0] - len(PEERS))
        elif kind == "S":
            select()
        elif kind == "E":
            expand(s)
            if len(marks) > 1:
                drain(marks.pop(1))
        if kind == "X":
            marks.append(len(sent) - 12)
    drain(len(sent))
    for one in stores:
        one.wait()


COPIES = 2 * (3 + 2 * 8 + 15 * 4) + 16 * (len(V_PARTS) + len(U_PARTS)) + 30


def local(incident, v_factors, u_factors, block_source, block_rank, block_slot, slot_target):
    anywhere, outside = pl.BlockSpec(memory_space=pl.ANY), pl.BlockSpec(memory_space=pltpu.HBM)
    return pl.pallas_call(
        kernel,
        out_shape=jax.ShapeDtypeStruct(incident.shape, jnp.bfloat16),
        in_specs=[outside] * 7,
        out_specs=anywhere,
        scratch_shapes=[
            pltpu.VMEM((CLUSTERS, PAD, CL), jnp.bfloat16),
            pltpu.VMEM((BLOCKS, PAD, 2 * GROUP), jnp.bfloat16),
            pltpu.VMEM((NZ, BLOCKS, GROUP, R), jnp.bfloat16),
            pltpu.VMEM((NZ, SLOTS, GROUP, R), jnp.bfloat16),
            pltpu.VMEM((BLOCKS, PAD, R), jnp.float32),
            pltpu.VMEM((BLOCKS, PAD, R), jnp.bfloat16),
            pltpu.VMEM((NC, PAD, R), jnp.bfloat16),
            pltpu.VMEM((NC, PAD, R), jnp.bfloat16),
            pltpu.VMEM((CLUSTERS * PAD, SLOTS * R), jnp.bfloat16),
            pltpu.VMEM((COLS, CLUSTERS * CL), jnp.bfloat16),
            pltpu.VMEM((NC, 16, 128), jnp.int32),
            pltpu.VMEM((NC, 16, 128), jnp.int32),
            pltpu.VMEM((BLOCKS * CLUSTERS, 16, 128), jnp.bfloat16),
            pltpu.VMEM((NC * BLOCKS, 16, 128), jnp.bfloat16),
            pltpu.VMEM((SLOTS * NC, 16, 128), jnp.bfloat16),
            pltpu.VMEM((SLOTS * CLUSTERS, 16, 128), jnp.bfloat16),
            pltpu.SMEM((BLOCKS,), jnp.int32),
            pltpu.SMEM((BLOCKS,), jnp.int32),
            pltpu.SMEM((BLOCKS,), jnp.int32),
            pltpu.SMEM((SLOTS,), jnp.int32),
            pltpu.SemaphoreType.DMA((COPIES,)),
            pltpu.SemaphoreType.DMA((COPIES,)),
            pltpu.SemaphoreType.DMA((13,)),
            pltpu.SemaphoreType.DMA((64,)),
        ],
        compiler_params=pltpu.CompilerParams(
            collective_id=0, has_side_effects=True, vmem_limit_bytes=60 * 1024 * 1024
        ),
        name="far_field",
    )(incident, v_factors, u_factors, block_source, block_rank, block_slot, slot_target)


def solution(mesh):
    torus = Mesh(mesh.devices.reshape(NZ, NX, NC), ("rhs_0", "rhs_1", "clus"))
    rhs = ("rhs_0", "rhs_1")
    return jax.shard_map(
        local,
        mesh=torus,
        in_specs=(
            P(rhs, "clus"),
            P("clus", rhs, None),
            P("clus", rhs, None),
            P("clus"),
            P("clus"),
            P("clus"),
            P("clus"),
        ),
        out_specs=P(rhs, "clus"),
        check_vma=False,
    )
```

time: 292 us -> 98.8 us (0.34)
  waiting for transfers between devices: 209 us -> 0 us
  Pallas kernels: 0 us -> 95.9 us
  matrix products: 22.9 us -> 0 us
  starting transfers between devices: 22.7 us -> 0 us
  blocking collectives: 14.1 us -> 0 us
  between operations: 13.5 us -> 0.01 us
  local copies, waits for them, and re-layouts: 7.7 us -> 2.75 us
    all_gather x2 -> x0, waiting for transfers between devices: 196 us -> none  [the longest x1 134 us: local(): lax.all_gather(u_factors, RHS, axis=1, tiled=True)]
    pallas_call x0 -> x1, Pallas kernels: none -> 95.9 us  [local(): pl.pallas_call(kernel, out_shape=jax.ShapeDtypeStruct(incident.shape, jnp...]
    dot_general x5 -> x0, matrix products: 22.9 us -> none  [the longest x1 13.1 us: local(): jnp.einsum('jt,jcr->ctr', owners, products, precision=lax.Precision.HIGHEST)]
    all_to_all x2 -> x0, starting transfers between devices: 22.7 us -> none  [the longest x1 15.4 us: local(): lax.all_to_all(labels, 'clus', split_axis=0, concat_axis=0, tiled=True)]
    all_gather x1 -> x0, blocking collectives: 14.1 us -> none  [whole_of(): whole = lax.all_gather(whole, axes[number], axis=dim, tiled=True)]
    all_to_all x2 -> x0, waiting for transfers between devices: 12.1 us -> none  [the longest x1 12.1 us: local(): lax.all_to_all(outgoing, 'clus', split_axis=0, concat_axis=0, tiled=True)]
  transfers between devices with their start and end apart: 4 -> 0, of which waited for: 3 -> 0; matrix products, arithmetic and copies ran while one was open for 4% -> 0% of each run, Pallas kernels for 0% -> 0%
where the time goes in v1:
time: 98.8 us; the launch traced here: 98.7 us
  Pallas kernels  95.9 us (97%)
  local copies, waits for them, and re-layouts  2.75 us (3%)
    pallas_call x1, Pallas kernels, local(): pl.pallas_call(kernel, out_shape=jax.ShapeDtypeStruct(incident.shape, jnp...  95.9 us
    unnamed x1, local copies, waits for them, and re-layouts  2.75 us

profile of v1, /device:TPU:8, one launch (start us, length us, event | category | flops | bytes accessed | tf_op | source)
XLA Modules:
  0.0 98.7 jit_solution(3291366640268722853)
XLA Ops:
  0.0 95.9 %far_field.1 = bf16[104,8192]{1,0:T(8,128)(2,1)} custom-call(bf16[104,8192]{1,0:T(8,128)(2,1)} %x_hbm.1, bf16[5,32,128]{2,1,0:T(8,128)(2,1)} %v_hbm.1, bf16[10,32,128]{2,1,0:T(8,128)(2,1)} %u_hbm.1, s32[5]{0:T(128)} %source_hbm.1, s32[5]{0:T(128)} %rank_hbm.1, s32[5]{0:T(128)} %slot_hbm.1, s32[10]{0:T(128)} %target_hbm.1), custom_call_target="tpu_custom_call" | custom-call | tf_op jit(solution)/shard_map/far_field/pallas_call | solution.py:386
  95.9 2.7 %copy.9 = bf16[104,8192]{1,0:T(8,128)(2,1)} copy(bf16[104,8192]{1,0:T(8,128)(2,1)} %far_field.1) | data formatting | bytes 3407872
